TPU v7x, 128 devices: a whole 4x4x4 slice. The times are simulated.
128 devices in a mesh: own: 8 (over y_lo, x), dp: 16 (over y_hi, z, core).
Axes of the slice: x: 4, y: 4 (y_hi: 2, y_lo: 2; y = y_hi * 2 + y_lo), z: 4, core: 2. Of those that a mesh axis runs over, the one named last changes fastest.
Arguments:
- tokens: bfloat16 [16384, 1536], P('dp'), may hold values from -6 to 6
- assign: int32 [128, 2], P('dp'), may hold values from 0 to 7, all different within a row; in each aligned block of 8 rows (0 to 7, 8 to 15, ...) at most 5 rows name the same one
- gates: float32 [16384, 2], P('dp'), may hold values from 0.25 to 1
- cot: bfloat16 [16384, 1536], P('dp', 'own'), may hold values from -1.75 to 1.75
- w_in: bfloat16 [8, 1536, 2048], P('own', None, 'dp'), may hold values from -0.15625 to 0.15625
- w_out: bfloat16 [8, 2048, 1536], P('own', 'dp'), may hold values from -0.125 to 0.125
Outputs:
- mixed: bfloat16 [16384, 1536], P('dp', 'own')
- grad_tokens: bfloat16 [16384, 1536], P('dp', 'own')
- grad_w_in: float32 [8, 1536, 2048], P('own', None, 'dp')
- grad_w_out: float32 [8, 2048, 1536], P('own', 'dp')
Inputs may be any that keep to these rules, and one draw needn't show every extreme that they name: `assign`: the two entries of a block name different experts. Among the 8 blocks of one index of dp no expert is named more than 5 times, and in every draw some expert is named exactly 5 times by the blocks of some index of dp.
All inputs are finite; a program needn't handle non-finite values.
Results may differ from a plain program's by a relative error of at most 0.012.
Values may be sent and summed in bfloat16 or wider, within the bound.
No kernel may reach another device: no remote copies, remote signals or barrier semaphores. Data moves between devices by JAX's collectives and lax.ppermute only.
A program may use at most 128 MiB of HBM per device.

v0:
```python
import jax
import jax.numpy as jnp
from jax import lax
from jax.sharding import PartitionSpec as P

CAP = 5


def pick_blocks(assign_rows, expert, capacity):
    hit_flag = jnp.logical_or(assign_rows[:, 0] == expert, assign_rows[:, 1] == expert).astype(
        jnp.int32
    )
    slot_rank = jnp.cumsum(hit_flag) - 1
    slot_ids = jnp.arange(capacity, dtype=jnp.int32)
    matches = jnp.logical_and(
        hit_flag[None, :] == 1, slot_rank[None, :] == slot_ids[:, None]
    ).astype(jnp.int32)
    where_idx = jnp.arange(assign_rows.shape[0], dtype=jnp.int32)
    blocks = jnp.sum(matches * where_idx[None, :], axis=1)
    is_valid = jnp.sum(matches, axis=1).astype(jnp.float32)
    return (blocks, is_valid)


def block_gates(assign_rows, gate_blocks, blocks, is_valid, expert):
    chosen = assign_rows[blocks]
    picked_gates = gate_blocks[blocks]
    first_hit = (chosen[:, 0] == expert).astype(jnp.float32)
    second_hit = (chosen[:, 1] == expert).astype(jnp.float32)
    mixing = picked_gates[..., 0] * first_hit[:, None] + picked_gates[..., 1] * second_hit[:, None]
    return mixing * is_valid[:, None]


def gelu_cdf(values):
    return 0.5 * (1.0 + jax.scipy.special.erf(values * 0.7071067811865476))


def gelu_slope(values):
    return gelu_cdf(values) + values * jnp.exp(-0.5 * values * values) * 0.3989422804014327


def place_rows(terms, blocks, block_count):
    block_len = terms.shape[-2]
    width = terms.shape[-1]
    zeros = jnp.zeros((block_count, block_len, width), jnp.float32)
    placed = zeros.at[blocks.reshape(-1)].add(terms.reshape(-1, block_len, width))
    return placed.reshape(block_count * block_len, width)


def body(tokens, assign, gates, cot, w_in, w_out):
    own_count = w_in.shape[0]
    block_count = assign.shape[0]
    block_len = tokens.shape[0] // block_count
    width = tokens.shape[1]
    full_in, full_out = (
        lax.all_gather(w_in, "dp", axis=2, tiled=True),
        lax.all_gather(w_out, "dp", axis=1, tiled=True),
    )
    expert_ids = lax.axis_index("own") * own_count + jnp.arange(own_count, dtype=jnp.int32)
    blocks, is_valid = jax.vmap(pick_blocks, (None, 0, None))(assign, expert_ids, CAP)
    gate_blocks = gates.reshape(block_count, block_len, 2)
    mixing = jax.vmap(block_gates, (None, None, 0, 0, 0))(
        assign, gate_blocks, blocks, is_valid, expert_ids
    )
    weight_rows = mixing.reshape(own_count, CAP * block_len)
    token_blocks = tokens.reshape(block_count, block_len, width)
    picked = token_blocks[blocks].reshape(own_count, CAP * block_len, width)
    pre_act = jnp.einsum("erd,edf->erf", picked, full_in, preferred_element_type=jnp.float32)
    hidden = (pre_act * gelu_cdf(pre_act)).astype(jnp.bfloat16)
    expert_out = jnp.einsum("erf,efd->erd", hidden, full_out, preferred_element_type=jnp.float32)
    contrib = (weight_rows[..., None] * expert_out).reshape(own_count, CAP, block_len, width)
    partial_rows = place_rows(contrib, blocks, block_count)
    mixed = lax.psum_scatter(
        partial_rows.astype(jnp.bfloat16), "own", scatter_dimension=1, tiled=True
    )
    cot_full = lax.all_gather(cot, "own", axis=1, tiled=True)
    cot_picked = cot_full.reshape(block_count, block_len, width)[blocks].reshape(
        own_count, CAP * block_len, width
    )
    grad_out = (weight_rows[..., None] * cot_picked.astype(jnp.float32)).astype(jnp.bfloat16)
    grad_hidden = jnp.einsum("erd,efd->erf", grad_out, full_out, preferred_element_type=jnp.float32)
    grad_pre = (grad_hidden * gelu_slope(pre_act)).astype(jnp.bfloat16)
    grad_in_terms = jnp.einsum(
        "erf,edf->erd", grad_pre, full_in, preferred_element_type=jnp.float32
    )
    grad_rows = place_rows(
        grad_in_terms.reshape(own_count, CAP, block_len, width), blocks, block_count
    )
    grad_tokens = lax.psum_scatter(
        grad_rows.astype(jnp.bfloat16), "own", scatter_dimension=1, tiled=True
    )
    out_full = jnp.einsum("erf,erd->efd", hidden, grad_out, preferred_element_type=jnp.float32)
    in_full = jnp.einsum("erf,erd->efd", grad_pre, picked, preferred_element_type=jnp.float32)
    grad_w_out, in_shard = (
        lax.psum_scatter(
            out_full.astype(jnp.bfloat16), "dp", scatter_dimension=1, tiled=True
        ).astype(jnp.float32),
        lax.psum_scatter(
            in_full.astype(jnp.bfloat16), "dp", scatter_dimension=1, tiled=True
        ).astype(jnp.float32),
    )
    grad_w_in = jnp.transpose(in_shard, (0, 2, 1))
    return (mixed, grad_tokens, grad_w_in, grad_w_out)


def solution(mesh):
    placed = (
        P("dp", None),
        P("dp", None),
        P("dp", None),
        P("dp", "own"),
        P("own", None, "dp"),
        P("own", "dp", None),
    )
    return jax.shard_map(
        body,
        mesh=mesh,
        in_specs=placed,
        out_specs=(P("dp", "own"), P("dp", "own"), P("own", None, "dp"), P("own", "dp", None)),
        check_vma=False,
    )
```

profile of v0, /device:TPU:0, one launch (start us, length us, event | category | flops | bytes accessed | tf_op | source)
XLA Modules:
  0.0 489.7 jit_solution(8797572180045873756)
XLA Ops:
  7.2 0.0 copy-start
  7.2 0.0 all-gather.8.cloned.1.call-start
  7.2 0.7 all-gather.8.cloned.1.call-update
  7.9 0.0 all-gather.4.cloned.1.call-start
  8.0 0.7 all-gather.4.cloned.1.call-update
  8.7 0.0 all-gather.6.cloned.1.call-start
  8.7 0.7 all-gather.6.cloned.1.call-update
  9.4 0.0 reduce-scatter.9.cloned.1.call-start
  9.4 0.8 copy.19
  10.2 0.8 compare_bitcast_fusion
  11.0 0.2 reduce-window.7
  11.2 0.3 convert_reduce_fusion
  11.4 0.6 gather_fusion.1
  12.0 0.1 copy.20
  12.1 1.3 gather_fusion
  13.4 0.0 copy-done
  13.4 2.2 gather_fusion.2
  15.6 0.1 broadcast_reduce_fusion
  15.7 0.1 broadcast_reduce_fusion.1
  15.8 40.3 %all-gather.8.cloned.1.call-done = bf16[1024,1536]{0,1:T(8,128)(2,1)} async-done(((bf16[1024,192]{0,1:T(8,128)(2,1)}), bf16[1024,1536]{0,1:T(8,128)(2,1)}) %all-gather.8.cloned.1.call-update) | async-done | bytes 3145744 | tf_op jit(solution)/shard_map/all_gather | solution.py:75
  56.1 3.2 copy.22
  59.3 2.1 gather_fusion.3
  61.4 63.2 %all-gather.4.cloned.1.call-done = bf16[1,1536,2048]{2,1,0:T(8,128)(2,1)} async-done(((bf16[1,1536,128]{2,1,0:T(8,128)(2,1)}), bf16[1,1536,2048]{2,1,0:T(8,128)(2,1)}) %all-gather.4.cloned.1.call-update) | async-done | bytes 6291472 | tf_op jit(solution)/shard_map/all_gather | solution.py:55
  124.6 0.0 copy-start.2
  124.6 9.2 %multiply_convert_fusion = (bf16[640,2048]{1,0:T(8,128)(2,1)}, f32[640,2048]{1,0:T(8,128)}) fusion(bf16[640,1536]{1,0:T(8,128)(2,1)} %bitcast.89, bf16[1,1536,2048]{2,1,0:T(8,128)(2,1)} %all-gather.4.cloned.1.call-done), kind=kOutput, calls=%fused_computation.25 | convolution fusion | flops 4033085440 | bytes 16121856 | tf_op jit(solution)/shard_map/erd,edf->erf/dot_general | solution.py:67
  133.8 54.6 %all-gather.6.cloned.1.call-done = bf16[1,2048,1536]{2,1,0:T(8,128)(2,1)} async-done(((bf16[1,128,1536]{2,1,0:T(8,128)(2,1)}), bf16[1,2048,1536]{2,1,0:T(8,128)(2,1)}) %all-gather.6.cloned.1.call-update) | async-done | bytes 6291472 | tf_op jit(solution)/shard_map/all_gather | solution.py:56
  188.5 0.0 copy-done.2
  188.5 0.0 copy-start.3
  188.5 8.4 %fusion.15 = bf16[640,2048]{1,0:T(8,128)(2,1)S(1)} fusion(f32[640,2048]{1,0:T(8,128)} %get-tuple-element.25, bf16[1,2048,1536]{2,1,0:T(8,128)(2,1)} %all-gather.6.cloned.1.call-done, f32[640]{0:T(1024)S(1)} %bitcast_multiply_fusion.1, bf16[1,640,1,1,1,1,1536]{6,1,5,4,3,2,0:T(8,128)(2,1)S(1)} %bitcast.87), kind=kOutput, calls=%fused_computation.24 | convolution fusion | flops 4042588160 | bytes 16124416 | tf_op jit(solution)/shard_map/erd,efd->erf/dot_general | solution.py:80
  196.9 0.0 copy-start.4
  196.9 1.6 copy-done.4
  198.4 0.0 copy-done.3
  198.4 7.0 %fusion = bf16[1,2048,1536]{2,1,0:T(8,128)(2,1)} fusion(bf16[640,2048]{1,0:T(8,128)(2,1)S(1)} %fusion.15, bf16[640,1536]{1,0:T(8,128)(2,1)S(1)} %bitcast.90), kind=kOutput, calls=%fused_computation.9 | convolution fusion | flops 4029677568 | bytes 10878976 | tf_op jit(solution)/shard_map/erf,erd->efd/dot_general | solution.py:92
  205.4 0.0 reduce-scatter.9.cloned.1.call-update
  205.5 0.0 reduce-scatter.11.cloned.1.call-start
  205.5 0.0 copy-start.6
  205.5 0.4 fusion.16
  205.9 1.3 copy-done.6
  207.3 7.0 %fusion.1 = bf16[1,2048,1536]{2,1,0:T(8,128)(2,1)} fusion(bf16[640,2048]{1,0:T(8,128)(2,1)S(1)} %copy-done.6, bf16[640,1536]{1,0:T(8,128)(2,1)S(1)} %fusion.16), kind=kOutput, calls=%fused_computation.10 | convolution fusion | flops 4029677568 | bytes 10878976 | tf_op jit(solution)/shard_map/erf,erd->efd/dot_general | solution.py:91
  214.2 0.0 copy-start.5
  214.2 0.0 reduce-scatter.11.cloned.1.call-update
  214.3 0.2 reduce-scatter.7.cloned.1.call-start
  214.5 1.7 copy-done.5
  216.2 9.4 %fusion.2 = f32[5,128,1536]{2,1,0:T(8,128)} fusion(bf16[5,128,2048]{2,1,0:T(8,128)(2,1)S(1)} %bitcast.92, bf16[1,1536,2048]{2,1,0:T(8,128)(2,1)} %all-gather.4.cloned.1.call-done), kind=kOutput, calls=%fused_computation.11 | convolution fusion | flops 4026531840 | bytes 12845056 | tf_op jit(solution)/shard_map/erf,edf->erd/dot_general | solution.py:82
  225.6 3.4 broadcast.269.clone.1
  229.0 10.4 %scatter_fusion.1 = f32[8,128,1536]{2,1,0:T(8,128)} fusion(f32[8,128,1536]{2,1,0:T(8,128)} %broadcast.269.clone.1, s32[5]{0:T(128)S(1)} %fusion.28, f32[5,128,1536]{2,1,0:T(8,128)} %fusion.2), kind=kCustom, calls=%fused_computation.5 | custom fusion | flops 983040 | bytes 11796500 | tf_op jit(solution)/shard_map/scatter-add | solution.py:45
  239.3 3.2 convert_element_type.158
  242.5 3.0 copy.23
  245.5 0.0 reduce-scatter.7.cloned.1.call-update
  245.5 0.0 reduce-scatter.5.cloned.1.call-start
  245.6 9.8 %fusion.17 = f32[640,1536]{1,0:T(8,128)} fusion(bf16[640,2048]{1,0:T(8,128)(2,1)} %get-tuple-element.24, bf16[1,2048,1536]{2,1,0:T(8,128)(2,1)} %all-gather.6.cloned.1.call-done, f32[640]{0:T(1024)S(1)} %bitcast_multiply_fusion.1), kind=kOutput, calls=%fused_computation.30 | convolution fusion | flops 4027514880 | bytes 12847616 | tf_op jit(solution)/shard_map/erf,efd->erd/dot_general | solution.py:69
  255.4 3.5 broadcast.269.clone
  258.8 10.4 %scatter_fusion = f32[8,128,1536]{2,1,0:T(8,128)} fusion(f32[8,128,1536]{2,1,0:T(8,128)} %broadcast.269.clone, s32[5]{0:T(128)S(1)} %fusion.28, f32[5,128,1536]{2,1,0:T(8,128)} %bitcast.88), kind=kCustom, calls=%fused_computation.4 | custom fusion | flops 983040 | bytes 11796500 | tf_op jit(solution)/shard_map/scatter-add | solution.py:45
  269.3 4.8 convert_element_type.151
  274.1 4.8 copy.21
  278.9 0.0 reduce-scatter.5.cloned.1.call-update
  278.9 14.3 %reduce-scatter.9.cloned.1.call-done = bf16[1,128,1536]{2,1,0:T(8,128)(2,1)} async-done(((bf16[1,2048,1536]{2,1,0:T(8,128)(2,1)}), bf16[1,128,1536]{2,1,0:T(8,128)(2,1)}) %reduce-scatter.9.cloned.1.call-update) | async-done | bytes 393232 | tf_op jit(solution)/shard_map/reduce_scatter | solution.py:97
  293.2 2.0 convert_bitcast_fusion
  295.2 2.3 copy.24
  297.5 88.5 %reduce-scatter.11.cloned.1.call-done = bf16[1,128,1536]{2,1,0:T(8,128)(2,1)} async-done(((bf16[1,2048,1536]{2,1,0:T(8,128)(2,1)}), bf16[1,128,1536]{2,1,0:T(8,128)(2,1)}) %reduce-scatter.11.cloned.1.call-update) | async-done | bytes 393232 | tf_op jit(solution)/shard_map/reduce_scatter | solution.py:94
  386.0 2.0 convert_element_type.167
  387.9 46.1 %reduce-scatter.7.cloned.1.call-done = bf16[1024,192]{0,1:T(8,128)(2,1)} async-done(((bf16[1024,1536]{0,1:T(8,128)(2,1)}), bf16[1024,192]{0,1:T(8,128)(2,1)}) %reduce-scatter.7.cloned.1.call-update) | async-done | bytes 393232 | tf_op jit(solution)/shard_map/reduce_scatter | solution.py:88
  434.0 48.8 %reduce-scatter.5.cloned.1.call-done = bf16[1024,192]{0,1:T(8,128)(2,1)} async-done(((bf16[1024,1536]{0,1:T(8,128)(2,1)}), bf16[1024,192]{0,1:T(8,128)(2,1)}) %reduce-scatter.5.cloned.1.call-update) | async-done | bytes 393232 | tf_op jit(solution)/shard_map/reduce_scatter | solution.py:72
  482.8 0.0 copy-done.1
  (9 shorter events, 0.1 us)
Async XLA Ops:
  7.2 6.2 %copy-start = (bf16[1024,1536]{1,0:T(8,128)(2,1)S(1)}, bf16[1024,1536]{1,0:T(8,128)(2,1)}, u32[]{:S(2)}) copy-start(bf16[1024,1536]{1,0:T(8,128)(2,1)} %param.6) | copy-start | bytes 9437188
  7.2 48.9 %all-gather.8.cloned.1.call-start = ((), (), s32[]{:S(2)}) async-start(), calls=%async_computation.7 | async-start | bytes 3538944 | tf_op jit(solution)/shard_map/all_gather | solution.py:75
  7.9 116.7 %all-gather.4.cloned.1.call-start = ((), (), s32[]{:S(2)}) async-start(), calls=%async_computation.4 | async-start | bytes 6684672 | tf_op jit(solution)/shard_map/all_gather | solution.py:55
  8.7 179.8 %all-gather.6.cloned.1.call-start = ((), (), s32[]{:S(2)}) async-start(), calls=%async_computation.5 | async-start | bytes 6684672 | tf_op jit(solution)/shard_map/all_gather | solution.py:56
  9.4 283.8 %reduce-scatter.9.cloned.1.call-start = ((), (), s32[]{:S(2)}) async-start(), calls=%async_computation.9 | async-start | bytes 6684672 | tf_op jit(solution)/shard_map/reduce_scatter | solution.py:97
  124.6 63.8 %copy-start.2 = (bf16[5,128,1536]{2,1,0:T(8,128)(2,1)S(1)}, bf16[5,128,1536]{2,1,0:T(8,128)(2,1)}, u32[]{:S(2)}) copy-start(bf16[5,128,1536]{2,1,0:T(8,128)(2,1)} %gather_fusion.3) | copy-start | bytes 5898244
  188.5 10.0 %copy-start.3 = (bf16[5,128,1536]{2,1,0:T(8,128)(2,1)S(1)}, bf16[5,128,1536]{2,1,0:T(8,128)(2,1)}, u32[]{:S(2)}) copy-start(bf16[5,128,1536]{2,1,0:T(8,128)(2,1)} %gather_fusion.2) | copy-start | bytes 5898244
  196.9 1.6 copy-start.4
  205.5 180.5 %reduce-scatter.11.cloned.1.call-start = ((), (), s32[]{:S(2)}) async-start(), calls=%async_computation.10 | async-start | bytes 6684672 | tf_op jit(solution)/shard_map/reduce_scatter | solution.py:94
  205.5 1.7 copy-start.6
  214.2 1.9 copy-start.5
  214.3 219.7 %reduce-scatter.7.cloned.1.call-start = ((), (), s32[]{:S(2)}) async-start(), calls=%async_computation.8 | async-start | bytes 3538944 | tf_op jit(solution)/shard_map/reduce_scatter | solution.py:88
  245.5 237.3 %reduce-scatter.5.cloned.1.call-start = ((), (), s32[]{:S(2)}) async-start(), calls=%async_computation.6 | async-start | bytes 3538944 | tf_op jit(solution)/shard_map/reduce_scatter | solution.py:72
  274.1 208.8 %copy-start.1 = (bf16[1024,1536]{1,0:T(8,128)(2,1)S(1)}, bf16[1024,1536]{1,0:T(8,128)(2,1)}, u32[]{:S(2)}) copy-start(bf16[1024,1536]{1,0:T(8,128)(2,1)} %param.6) | copy-start | bytes 9437188
Sparse Core Ops, SparseCore 0:
  9.6 46.3 all-gather.7
  58.3 66.2 all-gather.3
  127.1 61.2 all-gather.5
  205.6 87.5 reduce-scatter.8
  297.3 88.6 reduce-scatter.10
  388.8 45.1 reduce-scatter.6
  437.0 45.7 reduce-scatter.4
where the time goes:
time: 490 us
  waiting for transfers between devices  358 us (73%)
  matrix products  50.8 us (10%)
  other arithmetic  34.4 us (7%)
  local copies, waits for them, and re-layouts  31.9 us (7%)
  between operations  14.3 us (3%)
    reduce_scatter x1, waiting for transfers between devices, body(): lax.psum_scatter(out_full.astype(jnp.bfloat16), 'dp', scatter_dimension=1...  88.5 us
    all_gather x1, waiting for transfers between devices, body(): lax.all_gather(w_in, 'dp', axis=2, tiled=True)  63.2 us
    all_gather x1, waiting for transfers between devices, body(): lax.all_gather(w_out, 'dp', axis=1, tiled=True)  54.6 us
    reduce_scatter x1, waiting for transfers between devices, body(): lax.psum_scatter(partial_rows.astype(jnp.bfloat16), 'own', scatter_dimens...  48.8 us
    reduce_scatter x1, waiting for transfers between devices, body(): lax.psum_scatter(grad_rows.astype(jnp.bfloat16), 'own', scatter_dimension...  46.1 us
    all_gather x1, waiting for transfers between devices, body(): cot_full = lax.all_gather(cot, 'own', axis=1, tiled=True)  40.3 us
    scatter-add x2, other arithmetic, place_rows(): zeros.at[blocks.reshape(-1)].add(terms.reshape(-1, block_len, width))  20.8 us
    reduce_scatter x1, waiting for transfers between devices, body(): lax.psum_scatter(in_full.astype(jnp.bfloat16), 'dp', scatter_dimension=1,...  14.3 us
  transfers between devices with their start and end apart: 7, of which 7 were waited for; matrix products, arithmetic and copies ran while one was open for 20% of the time, Pallas kernels for 0%

commit v1 on v0

--- a/solution.py
+++ b/solution.py
@@ -72,7 +72,10 @@
     mixed = lax.psum_scatter(
         partial_rows.astype(jnp.bfloat16), "own", scatter_dimension=1, tiled=True
     )
-    cot_full = lax.all_gather(cot, "own", axis=1, tiled=True)
+    peers = lax.axis_size("own")
+    tiles = jnp.stack([cot for _ in range(peers)])
+    tiles = lax.all_to_all(tiles, "own", split_axis=0, concat_axis=0)
+    cot_full = jnp.concatenate(tiles, axis=1)
     cot_picked = cot_full.reshape(block_count, block_len, width)[blocks].reshape(
         own_count, CAP * block_len, width
     )

time: 490 us -> 473 us (0.965)
  waiting for transfers between devices: 358 us -> 330 us
  starting transfers between devices: 0.46 us -> 6.2 us
  local copies, waits for them, and re-layouts: 31.9 us -> 37 us
    all_gather x1 -> x0, waiting for transfers between devices: 40.3 us -> none  [body(): cot_full = lax.all_gather(cot, 'own', axis=1, tiled=True)]
    all_to_all x0 -> x1, waiting for transfers between devices: none -> 35.9 us  [body(): tiles = lax.all_to_all(tiles, 'own', split_axis=0, concat_axis=0)]
    all_gather x1, waiting for transfers between devices: 63.2 us -> 40.5 us  [body(): lax.all_gather(w_in, 'dp', axis=2, tiled=True)]
    another operation x2 -> x4, local copies, waits for them, and re-layouts: 6.83 us -> 13.3 us
    all_to_all x0 -> x1, starting transfers between devices: none -> 5.56 us  [body(): tiles = lax.all_to_all(tiles, 'own', split_axis=0, concat_axis=0)]
    unnamed x16 -> x19, local copies, waits for them, and re-layouts: 7.64 us -> 9.86 us
  transfers between devices with their start and end apart: 7 -> 7, of which waited for: 7 -> 7; matrix products, arithmetic and copies ran while one was open for 20% -> 21% of each run, Pallas kernels for 0% -> 0%
where the time goes in v1:
time: 473 us; the launch traced here: 472 us
  waiting for transfers between devices  330 us (70%)
  matrix products  50.6 us (11%)
  local copies, waits for them, and re-layouts  37 us (8%)
  other arithmetic  33.7 us (7%)
  between operations  14.3 us (3%)
  starting transfers between devices  6.2 us (1%)
    reduce_scatter x1, waiting for transfers between devices, body(): lax.psum_scatter(out_full.astype(jnp.bfloat16), 'dp', scatter_dimension=1...  88.5 us
    all_gather x1, waiting for transfers between devices, body(): lax.all_gather(w_out, 'dp', axis=1, tiled=True)  54.8 us
    reduce_scatter x1, waiting for transfers between devices, body(): lax.psum_scatter(partial_rows.astype(jnp.bfloat16), 'own', scatter_dimens...  49.3 us
    reduce_scatter x1, waiting for transfers between devices, body(): lax.psum_scatter(grad_rows.astype(jnp.bfloat16), 'own', scatter_dimension...  46.1 us
    all_gather x1, waiting for transfers between devices, body(): lax.all_gather(w_in, 'dp', axis=2, tiled=True)  40.5 us
    all_to_all x1, waiting for transfers between devices, body(): tiles = lax.all_to_all(tiles, 'own', split_axis=0, concat_axis=0)  35.9 us
    scatter-add x2, other arithmetic, place_rows(): zeros.at[blocks.reshape(-1)].add(terms.reshape(-1, block_len, width))  20.9 us
    reduce_scatter x1, waiting for transfers between devices, body(): lax.psum_scatter(in_full.astype(jnp.bfloat16), 'dp', scatter_dimension=1,...  13.8 us
  transfers between devices with their start and end apart: 7, of which 7 were waited for; matrix products, arithmetic and copies ran while one was open for 21% of the time, Pallas kernels for 0%

profile of v1, /device:TPU:0, one launch (start us, length us, event | category | flops | bytes accessed | tf_op | source)
XLA Modules:
  0.0 472.0 jit_solution(17091913122571755837)
XLA Ops:
  7.2 0.0 copy-start
  7.2 0.0 all-gather.3.cloned.1.call-start
  7.2 0.7 all-gather.3.cloned.1.call-update
  7.9 0.0 all-gather.5.cloned.1.call-start
  8.0 0.7 all-gather.5.cloned.1.call-update
  8.7 3.0 stack.2
  11.7 0.0 copy-start.4
  11.7 0.0 copy-start.2
  11.7 5.6 %all-to-all-start = ((bf16[8,1024,192]{1,2,0:T(8,128)(2,1)}), bf16[8,1024,192]{1,2,0:T(8,128)(2,1)}, u32[]{:S(2)}, u32[]{:S(2)}) async-start(bf16[8,1024,192]{1,2,0:T(8,128)(2,1)} %stack.2), calls=%async_computation.1 | async-start | bytes 6291456 | tf_op jit(solution)/shard_map/all_to_all | solution.py:77
  17.2 0.0 reduce-scatter.9.cloned.1.call-start
  17.3 0.0 copy-done.4
  17.3 0.1 copy.26
  17.4 0.2 reduce-window.7
  17.6 0.3 convert_reduce_fusion
  17.9 0.6 gather_fusion.1
  18.4 0.1 copy.27
  18.5 0.0 copy-done.2
  18.5 0.6 gather_fusion
  19.1 0.0 copy-done
  19.1 2.1 gather_fusion.2
  21.2 0.1 broadcast_reduce_fusion
  21.4 0.1 broadcast_reduce_fusion.1
  21.5 35.9 %all-to-all-done = bf16[8,1024,192]{1,2,0:T(8,128)(2,1)} async-done(((bf16[8,1024,192]{1,2,0:T(8,128)(2,1)}), bf16[8,1024,192]{1,2,0:T(8,128)(2,1)}, u32[]{:S(2)}, u32[]{:S(2)}) %all-to-all-start) | async-done | bytes 3145760 | tf_op jit(solution)/shard_map/all_to_all | solution.py:77
  57.4 2.7 copy.32
  60.1 3.4 copy.29
  63.5 2.6 gather_fusion.3
  66.1 40.5 %all-gather.3.cloned.1.call-done = bf16[1,1536,2048]{2,1,0:T(8,128)(2,1)} async-done(((bf16[1,1536,128]{2,1,0:T(8,128)(2,1)}), bf16[1,1536,2048]{2,1,0:T(8,128)(2,1)}) %all-gather.3.cloned.1.call-update) | async-done | bytes 6291472 | tf_op jit(solution)/shard_map/all_gather | solution.py:55
  106.5 9.1 %multiply_convert_fusion = (bf16[640,2048]{1,0:T(8,128)(2,1)}, f32[640,2048]{1,0:T(8,128)}) fusion(bf16[640,1536]{1,0:T(8,128)(2,1)} %bitcast.94, bf16[1,1536,2048]{2,1,0:T(8,128)(2,1)} %all-gather.3.cloned.1.call-done), kind=kOutput, calls=%fused_computation.25 | convolution fusion | flops 4033085440 | bytes 16121856 | tf_op jit(solution)/shard_map/erd,edf->erf/dot_general | solution.py:67
  115.6 54.8 %all-gather.5.cloned.1.call-done = bf16[1,2048,1536]{2,1,0:T(8,128)(2,1)} async-done(((bf16[1,128,1536]{2,1,0:T(8,128)(2,1)}), bf16[1,2048,1536]{2,1,0:T(8,128)(2,1)}) %all-gather.5.cloned.1.call-update) | async-done | bytes 6291472 | tf_op jit(solution)/shard_map/all_gather | solution.py:56
  170.4 8.4 %fusion.15 = bf16[640,2048]{1,0:T(8,128)(2,1)S(1)} fusion(f32[640,2048]{1,0:T(8,128)} %get-tuple-element.29, bf16[1,2048,1536]{2,1,0:T(8,128)(2,1)} %all-gather.5.cloned.1.call-done, f32[640]{0:T(1024)S(1)} %bitcast_multiply_fusion.1, bf16[1,640,1,1,1,1,1536]{6,1,5,4,3,2,0:T(8,128)(2,1)S(1)} %bitcast.92), kind=kOutput, calls=%fused_computation.24 | convolution fusion | flops 4042588160 | bytes 16124416 | tf_op jit(solution)/shard_map/erd,efd->erf/dot_general | solution.py:83
  178.7 0.0 copy-start.5
  178.8 1.6 copy-done.5
  180.3 0.0 copy-done.3
  180.3 7.0 %fusion = bf16[1,2048,1536]{2,1,0:T(8,128)(2,1)} fusion(bf16[640,2048]{1,0:T(8,128)(2,1)S(1)} %fusion.15, bf16[640,1536]{1,0:T(8,128)(2,1)S(1)} %bitcast.95), kind=kOutput, calls=%fused_computation.9 | convolution fusion | flops 4029677568 | bytes 10878976 | tf_op jit(solution)/shard_map/erf,erd->efd/dot_general | solution.py:95
  187.3 0.0 reduce-scatter.9.cloned.1.call-update
  187.4 0.2 reduce-scatter.11.cloned.1.call-start
  187.6 0.0 copy-start.7
  187.6 0.4 fusion.16
  188.0 1.3 copy-done.7
  189.3 7.0 %fusion.1 = bf16[1,2048,1536]{2,1,0:T(8,128)(2,1)} fusion(bf16[640,2048]{1,0:T(8,128)(2,1)S(1)} %copy-done.7, bf16[640,1536]{1,0:T(8,128)(2,1)S(1)} %fusion.16), kind=kOutput, calls=%fused_computation.10 | convolution fusion | flops 4029677568 | bytes 10878976 | tf_op jit(solution)/shard_map/erf,erd->efd/dot_general | solution.py:94
  196.3 0.0 reduce-scatter.11.cloned.1.call-update
  196.3 0.0 reduce-scatter.7.cloned.1.call-start
  196.4 1.9 copy-done.6
  198.2 9.4 %fusion.2 = f32[5,128,1536]{2,1,0:T(8,128)} fusion(bf16[5,128,2048]{2,1,0:T(8,128)(2,1)S(1)} %bitcast.97, bf16[1,1536,2048]{2,1,0:T(8,128)(2,1)} %all-gather.3.cloned.1.call-done), kind=kOutput, calls=%fused_computation.11 | convolution fusion | flops 4026531840 | bytes 12845056 | tf_op jit(solution)/shard_map/erf,edf->erd/dot_general | solution.py:85
  207.7 3.4 broadcast.271.clone.1
  211.0 10.4 %scatter_fusion.1 = f32[8,128,1536]{2,1,0:T(8,128)} fusion(f32[8,128,1536]{2,1,0:T(8,128)} %broadcast.271.clone.1, s32[5]{0:T(128)S(1)} %fusion.28, f32[5,128,1536]{2,1,0:T(8,128)} %fusion.2), kind=kCustom, calls=%fused_computation.5 | custom fusion | flops 983040 | bytes 11796500 | tf_op jit(solution)/shard_map/scatter-add | solution.py:45
  221.4 3.2 convert_element_type.158
  224.6 3.0 copy.30
  227.6 0.0 reduce-scatter.7.cloned.1.call-update
  227.6 0.3 reduce-scatter.5.cloned.1.call-start
  227.9 9.8 %fusion.17 = f32[640,1536]{1,0:T(8,128)} fusion(bf16[640,2048]{1,0:T(8,128)(2,1)} %get-tuple-element.28, bf16[1,2048,1536]{2,1,0:T(8,128)(2,1)} %all-gather.5.cloned.1.call-done, f32[640]{0:T(1024)S(1)} %bitcast_multiply_fusion.1), kind=kOutput, calls=%fused_computation.30 | convolution fusion | flops 4027514880 | bytes 12847616 | tf_op jit(solution)/shard_map/erf,efd->erd/dot_general | solution.py:69
  237.7 3.5 broadcast.271.clone
  241.1 10.6 %scatter_fusion = f32[8,128,1536]{2,1,0:T(8,128)} fusion(f32[8,128,1536]{2,1,0:T(8,128)} %broadcast.271.clone, s32[5]{0:T(128)S(1)} %fusion.28, f32[5,128,1536]{2,1,0:T(8,128)} %bitcast.93), kind=kCustom, calls=%fused_computation.4 | custom fusion | flops 983040 | bytes 11796500 | tf_op jit(solution)/shard_map/scatter-add | solution.py:45
  251.7 4.8 %convert_element_type.151 = bf16[8,128,1536]{2,1,0:T(8,128)(2,1)} convert(f32[8,128,1536]{2,1,0:T(8,128)} %scatter_fusion) | non-fusion elementwise | flops 1572864 | bytes 9437184 | tf_op jit(solution)/shard_map/convert_element_type | solution.py:73
  256.4 4.9 %copy.28 = bf16[1024,1536]{0,1:T(8,128)(2,1)} copy(bf16[1024,1536]{1,0:T(8,128)(2,1)} %bitcast.91) | data formatting | bytes 6291456 | tf_op jit(solution)/shard_map/convert_element_type | solution.py:73
  261.3 0.0 reduce-scatter.5.cloned.1.call-update
  261.3 13.8 %reduce-scatter.9.cloned.1.call-done = bf16[1,128,1536]{2,1,0:T(8,128)(2,1)} async-done(((bf16[1,2048,1536]{2,1,0:T(8,128)(2,1)}), bf16[1,128,1536]{2,1,0:T(8,128)(2,1)}) %reduce-scatter.9.cloned.1.call-update) | async-done | bytes 393232 | tf_op jit(solution)/shard_map/reduce_scatter | solution.py:100
  275.1 2.0 convert_bitcast_fusion
  277.1 2.3 copy.31
  279.3 88.5 %reduce-scatter.11.cloned.1.call-done = bf16[1,128,1536]{2,1,0:T(8,128)(2,1)} async-done(((bf16[1,2048,1536]{2,1,0:T(8,128)(2,1)}), bf16[1,128,1536]{2,1,0:T(8,128)(2,1)}) %reduce-scatter.11.cloned.1.call-update) | async-done | bytes 393232 | tf_op jit(solution)/shard_map/reduce_scatter | solution.py:97
  367.8 2.0 convert_element_type.167
  369.8 46.1 %reduce-scatter.7.cloned.1.call-done = bf16[1024,192]{0,1:T(8,128)(2,1)} async-done(((bf16[1024,1536]{0,1:T(8,128)(2,1)}), bf16[1024,192]{0,1:T(8,128)(2,1)}) %reduce-scatter.7.cloned.1.call-update) | async-done | bytes 393232 | tf_op jit(solution)/shard_map/reduce_scatter | solution.py:91
  415.9 49.3 %reduce-scatter.5.cloned.1.call-done = bf16[1024,192]{0,1:T(8,128)(2,1)} async-done(((bf16[1024,1536]{0,1:T(8,128)(2,1)}), bf16[1024,192]{0,1:T(8,128)(2,1)}) %reduce-scatter.5.cloned.1.call-update) | async-done | bytes 393232 | tf_op jit(solution)/shard_map/reduce_scatter | solution.py:72
  465.1 0.0 copy-done.1
  (12 shorter events, 0.1 us)
Async XLA Ops:
  7.2 12.0 %copy-start = (bf16[1024,1536]{1,0:T(8,128)(2,1)S(1)}, bf16[1024,1536]{1,0:T(8,128)(2,1)}, u32[]{:S(2)}) copy-start(bf16[1024,1536]{1,0:T(8,128)(2,1)} %param.6) | copy-start | bytes 9437188
  7.2 99.4 %all-gather.3.cloned.1.call-start = ((), (), s32[]{:S(2)}) async-start(), calls=%async_computation.5 | async-start | bytes 6684672 | tf_op jit(solution)/shard_map/all_gather | solution.py:55
  7.9 162.4 %all-gather.5.cloned.1.call-start = ((), (), s32[]{:S(2)}) async-start(), calls=%async_computation.6 | async-start | bytes 6684672 | tf_op jit(solution)/shard_map/all_gather | solution.py:56
  11.7 5.6 %copy-start.4 = (s32[8,2]{0,1:T(2,128)S(1)}, s32[8,2]{0,1:T(2,128)}, u32[]{:S(2)}) copy-start(s32[8,2]{0,1:T(2,128)} %param.7) | copy-start | bytes 196
  11.7 6.8 %copy-start.2 = (f32[1024,2]{0,1:T(2,128)S(1)}, f32[1024,2]{0,1:T(2,128)}, u32[]{:S(2)}) copy-start(f32[1024,2]{0,1:T(2,128)} %param.8) | copy-start | bytes 24580
  11.7 45.7 %all-to-all-start = ((bf16[8,1024,192]{1,2,0:T(8,128)(2,1)}), bf16[8,1024,192]{1,2,0:T(8,128)(2,1)}, u32[]{:S(2)}, u32[]{:S(2)}) async-start(bf16[8,1024,192]{1,2,0:T(8,128)(2,1)} %stack.2), calls=%async_computation.1 | async-start | bytes 6291456 | tf_op jit(solution)/shard_map/all_to_all | solution.py:77
  17.2 257.9 %reduce-scatter.9.cloned.1.call-start = ((), (), s32[]{:S(2)}) async-start(), calls=%async_computation.9 | async-start | bytes 6684672 | tf_op jit(solution)/shard_map/reduce_scatter | solution.py:100
  170.3 10.0 %copy-start.3 = (bf16[5,128,1536]{2,1,0:T(8,128)(2,1)S(1)}, bf16[5,128,1536]{2,1,0:T(8,128)(2,1)}, u32[]{:S(2)}) copy-start(bf16[5,128,1536]{2,1,0:T(8,128)(2,1)} %gather_fusion.2) | copy-start | bytes 5898244
  178.7 1.6 copy-start.5
  187.4 180.5 %reduce-scatter.11.cloned.1.call-start = ((), (), s32[]{:S(2)}) async-start(), calls=%async_computation.10 | async-start | bytes 6684672 | tf_op jit(solution)/shard_map/reduce_scatter | solution.py:97
  187.6 1.7 copy-start.7
  196.3 1.9 copy-start.6
  196.3 219.5 %reduce-scatter.7.cloned.1.call-start = ((), (), s32[]{:S(2)}) async-start(), calls=%async_computation.8 | async-start | bytes 3538944 | tf_op jit(solution)/shard_map/reduce_scatter | solution.py:91
  227.6 237.5 %reduce-scatter.5.cloned.1.call-start = ((), (), s32[]{:S(2)}) async-start(), calls=%async_computation.7 | async-start | bytes 3538944 | tf_op jit(solution)/shard_map/reduce_scatter | solution.py:72
  256.4 208.7 %copy-start.1 = (bf16[1024,1536]{1,0:T(8,128)(2,1)S(1)}, bf16[1024,1536]{1,0:T(8,128)(2,1)}, u32[]{:S(2)}) copy-start(bf16[1024,1536]{1,0:T(8,128)(2,1)} %param.6) | copy-start | bytes 9437188
Sparse Core Ops, SparseCore 0:
  10.3 96.2 all-gather.2
  109.0 61.2 all-gather.4
  187.5 87.5 reduce-scatter.8
  279.1 88.6 reduce-scatter.10
  370.7 45.1 reduce-scatter.6
  418.7 46.3 reduce-scatter.4
